TPU v7x, 256 devices: a whole 4x4x8 slice. The times are simulated.
256 devices in a mesh: seq: 64 (over x, y_lo, z), ch: 4 (over y_hi, core).
Axes of the slice: x: 4, y: 4 (y_hi: 2, y_lo: 2; y = y_hi * 2 + y_lo), z: 8, core: 2. Of those that a mesh axis runs over, the one named last changes fastest.
Arguments:
- projected: bfloat16 [8192, 3, 4096], P('seq', None, 'ch'), may hold values from -6 to 6
- cotangent: bfloat16 [8192, 4096], P('seq', 'ch'), may hold values from -6 to 6
- short_weight: float32 [3, 7, 4096], P(None, None, 'ch'), may hold values from -2 to 2
- long_filter: float32 [8, 8192], P('ch', 'seq'), may hold values from -0.0625 to 0.0625
Outputs:
- grad_proj: bfloat16 [8192, 3, 4096], P('seq', None, 'ch')
- grad_short: float32 [3, 7, 4096], P(None, None, 'ch')
- grad_filter: float32 [8, 8192], P(None, ('seq', 'ch'))
All inputs are finite; a program needn't handle non-finite values.
Results may differ from a plain program's by a relative error of at most 0.00155.
Values may be sent and summed in bfloat16 or wider, within the bound.
No kernel may reach another device: no remote copies, remote signals or barrier semaphores. Data moves between devices by JAX's collectives and lax.ppermute only.
A program may use at most 64 MiB of HBM per device.

v0:
```python
import math
import jax
import jax.numpy as jnp
from jax import lax
from jax.sharding import PartitionSpec as P

highest = lax.Precision.HIGHEST


def passed_along(block, axis, distance):
    devices = range(lax.axis_size(axis))
    route = [(i - distance, i) for i in devices if i - distance in devices]
    return lax.ppermute(block, axis, route)


def einsum_high(form, table, operand):
    return jnp.einsum(form, table, operand, precision=highest)


def angle_table(first, second, length):
    product = first[:, None] * second[None, :] % length
    radians = product.astype(jnp.float32) * (2.0 * math.pi / length)
    return (jnp.cos(radians), jnp.sin(radians))


def complex_dft(cosine, sine, real_part, imag_part, joined, sign):
    table = jnp.stack(
        [jnp.stack([cosine, -sign * sine], 0), jnp.stack([sign * sine, cosine], 0)], 0
    )
    stacked = jnp.stack([real_part, imag_part], 0)
    result = jnp.einsum(joined, table, stacked, precision=highest)
    return (result[0], result[1])


def rotate(real_part, imag_part, cosine, sine, sign):
    return (
        real_part * cosine - sign * imag_part * sine,
        imag_part * cosine + sign * real_part * sine,
    )


def combine(mixed_re, mixed_im, grad_re, grad_im, filt_re, filt_im):
    conv_re = filt_re * mixed_re - filt_im * mixed_im
    conv_im = filt_re * mixed_im + filt_im * mixed_re
    corr_re = filt_re * grad_re + filt_im * grad_im
    corr_im = filt_re * grad_im - filt_im * grad_re
    cross_re = mixed_re * grad_re + mixed_im * grad_im
    cross_im = mixed_re * grad_im - mixed_im * grad_re
    return (conv_re - corr_im, conv_im + corr_re, cross_re, cross_im)


def featurize(extended, weights, row_count):
    tap_count = weights.shape[1]
    accumulated = jnp.zeros((row_count,) + extended.shape[1:], jnp.float32)
    for offset in range(tap_count):
        first_row = tap_count - 1 - offset
        accumulated = accumulated + weights[:, offset, :] * extended[
            first_row : first_row + row_count
        ].astype(jnp.float32)
    return accumulated


def transpose_pair(signals, filters):
    return (
        lax.all_to_all(signals, "seq", split_axis=0, concat_axis=1, tiled=True),
        lax.all_to_all(filters, "seq", split_axis=0, concat_axis=1, tiled=True),
    )


def sequence_plan(mixed_input, gated_grad, long_filter):
    row_count, chan_count = mixed_input.shape
    group_count = long_filter.shape[0]
    seq_count = lax.axis_size("seq")
    seq_index = lax.axis_index("seq")
    per_block = row_count // seq_count
    fft_length = 2 * row_count * seq_count
    freq_index = jnp.arange(2 * seq_count, dtype=jnp.int32)
    block_index = jnp.arange(seq_count, dtype=jnp.int32)
    row_index = jnp.arange(row_count, dtype=jnp.int32)
    signals = jnp.stack([mixed_input, gated_grad], 1)[:, None]
    filters = jnp.transpose(long_filter)[:, None]
    sig_cols, filt_cols = transpose_pair(signals, filters)
    cos_one, sin_one = angle_table(freq_index, block_index, 2 * seq_count)
    sig_re = einsum_high("kb,abxc->kaxc", cos_one, sig_cols)
    sig_im = -einsum_high("kb,abxc->kaxc", sin_one, sig_cols)
    filt_re = einsum_high("kb,abg->kag", cos_one, filt_cols)
    filt_im = -einsum_high("kb,abg->kag", sin_one, filt_cols)
    positions = seq_index * per_block + jnp.arange(per_block, dtype=jnp.int32)
    cos_twist, sin_twist = angle_table(freq_index, positions, fft_length)
    sig_re, sig_im = rotate(
        sig_re, sig_im, cos_twist[:, :, None, None], sin_twist[:, :, None, None], -1.0
    )
    filt_re, filt_im = rotate(filt_re, filt_im, cos_twist[:, :, None], sin_twist[:, :, None], -1.0)
    sig_rows, filt_rows = transpose_pair(
        jnp.stack([sig_re, sig_im], 2), jnp.stack([filt_re, filt_im], 2)
    )
    cos_two, sin_two = angle_table(row_index, row_index, row_count)
    spec_re, spec_im = complex_dft(
        cos_two, sin_two, sig_rows[:, :, 0], sig_rows[:, :, 1], "pqka,qjaxc->pjkxc", -1.0
    )
    hspec_re, hspec_im = complex_dft(
        cos_two, sin_two, filt_rows[:, :, 0], filt_rows[:, :, 1], "pqka,qjag->pjkg", -1.0
    )
    leading = spec_re.shape[:2]
    group_shape = leading + (group_count, chan_count // group_count)
    wave_re, wave_im, cross_re, cross_im = combine(
        spec_re[:, :, 0].reshape(group_shape),
        spec_im[:, :, 0].reshape(group_shape),
        spec_re[:, :, 1].reshape(group_shape),
        spec_im[:, :, 1].reshape(group_shape),
        hspec_re[..., None],
        hspec_im[..., None],
    )
    wave_re = wave_re.reshape(leading + (chan_count,))
    wave_im = wave_im.reshape(leading + (chan_count,))
    cross_re = jnp.sum(cross_re, -1)
    cross_im = jnp.sum(cross_im, -1)
    back_re, back_im = complex_dft(cos_two, sin_two, wave_re, wave_im, "pqak,qjkc->pajc", 1.0)
    cback_re, cback_im = complex_dft(cos_two, sin_two, cross_re, cross_im, "pqak,qjkg->pajg", 1.0)
    pair_freq = seq_index * 2 + jnp.arange(2, dtype=jnp.int32)
    cos_back, sin_back = angle_table(row_index, pair_freq, fft_length)
    back_re, back_im = rotate(back_re, back_im, cos_back[:, :, None], sin_back[:, :, None], 1.0)
    cback_re, cback_im = rotate(cback_re, cback_im, cos_back[:, :, None], sin_back[:, :, None], 1.0)
    wave_cols, cross_cols = transpose_pair(
        jnp.stack([back_re, back_im], 2), jnp.stack([cback_re, cback_im], 2)
    )
    cos_three, sin_three = angle_table(block_index, freq_index, 2 * seq_count)
    time_re, time_im = complex_dft(
        cos_three, sin_three, wave_cols[:, :, 0], wave_cols[:, :, 1], "pqbk,qakc->pbac", 1.0
    )
    cross_time = einsum_high("bk,akg->bag", cos_three, cross_cols[:, :, 0]) - einsum_high(
        "bk,akg->bag", sin_three, cross_cols[:, :, 1]
    )
    inverse_scale = 1.0 / fft_length
    wave_out, cross_out = transpose_pair(
        jnp.stack([time_re, time_im], 2) * inverse_scale, cross_time * inverse_scale
    )
    return (wave_out[0, :, 0], wave_out[0, :, 1], jnp.transpose(cross_out[0]))


def local(projected, cotangent, short_weight, long_filter):
    tap_count = short_weight.shape[1]
    row_count = projected.shape[0]
    margin = tap_count - 1
    front_rows = passed_along(projected[row_count - margin :], "seq", 1)
    extended = jnp.concatenate([front_rows, projected], 0)
    features = featurize(extended, short_weight, row_count)
    grad_out = cotangent.astype(jnp.float32)
    mixed_input = features[:, 1] * features[:, 2]
    gated_grad = grad_out * features[:, 0]
    conv_out, corr_out, filt_grad = sequence_plan(mixed_input, gated_grad, long_filter)
    token_count = row_count * lax.axis_size("seq")
    group_width = mixed_input.shape[1] // long_filter.shape[0]
    scaled_grad = filt_grad * (1.0 / math.sqrt(token_count * group_width))
    owned_grad = lax.all_to_all(scaled_grad, "ch", split_axis=1, concat_axis=0, tiled=True)
    feat_grad = jnp.stack(
        [grad_out * conv_out, corr_out * features[:, 2], corr_out * features[:, 1]], 1
    )
    next_rows = passed_along(feat_grad[:margin].astype(jnp.bfloat16), "seq", -1).astype(jnp.float32)
    extended_grad = jnp.concatenate([feat_grad, next_rows], 0)
    grad_proj = jnp.zeros(feat_grad.shape, jnp.float32)
    for offset in range(tap_count):
        grad_proj = (
            grad_proj + short_weight[:, offset, :] * extended_grad[offset : offset + row_count]
        )
    short_terms = []
    for offset in range(tap_count):
        first_row = margin - offset
        short_terms.append(
            jnp.sum(feat_grad * extended[first_row : first_row + row_count].astype(jnp.float32), 0)
        )
    grad_short = lax.psum(jnp.stack(short_terms, 1), "seq") * (1.0 / math.sqrt(token_count))
    return (grad_proj.astype(jnp.bfloat16), grad_short, owned_grad)


def solution(mesh):
    return jax.shard_map(
        local,
        mesh=mesh,
        in_specs=(P("seq", None, "ch"), P("seq", "ch"), P(None, None, "ch"), P("ch", "seq")),
        out_specs=(P("seq", None, "ch"), P(None, None, "ch"), P(None, ("seq", "ch"))),
        check_vma=False,
    )
```

profile of v0, /device:TPU:16, one launch (start us, length us, event | category | flops | bytes accessed | tf_op | source)
XLA Modules:
  0.0 929.5 jit_solution(14938506437671617002)
XLA Ops:
  8.1 3.8 collective-permute-start
  13.4 11.8 %all-to-all-start = ((f32[128,1,2]{2,1,0:T(1,128)}), f32[128,1,2]{2,1,0:T(1,128)S(1)}, u32[]{:S(2)}, u32[]{:S(2)}) async-start(f32[128,1,2]{2,1,0:T(1,128)} %bitcast.9), calls=%async_computation | async-start | bytes 131072 | tf_op jit(solution)/shard_map/all_to_all | solution.py:66
  28.6 5.6 fusion.9
  38.0 11.2 %all-to-all-start.2 = ((f32[128,1,2,1024]{3,2,1,0:T(2,128)}), f32[128,1,2,1024]{3,2,1,0:T(2,128)S(1)}, u32[]{:S(2)}, u32[]{:S(2)}) async-start(f32[128,1,2,1024]{3,2,1,0:T(2,128)} %copy.147), calls=%async_computation.2 | async-start | bytes 2097152 | tf_op jit(solution)/shard_map/all_to_all | solution.py:65
  51.5 25.5 %all-to-all-done.2 = f32[128,1,2,1024]{3,2,1,0:T(2,128)S(1)} async-done(((f32[128,1,2,1024]{3,2,1,0:T(2,128)}), f32[128,1,2,1024]{3,2,1,0:T(2,128)S(1)}, u32[]{:S(2)}, u32[]{:S(2)}) %all-to-all-start.2) | async-done | bytes 1048608 | tf_op jit(solution)/shard_map/all_to_all | solution.py:65
  77.1 6.5 all-to-all-start.1
  89.4 5.2 copy.149
  95.8 10.6 %all-to-all-start.3 = ((f32[128,2,2,2,1024]{4,3,1,2,0:T(2,128)}), f32[128,2,2,2,1024]{4,3,1,2,0:T(2,128)}, u32[]{:S(2)}, u32[]{:S(2)}) async-start(f32[128,2,2,2,1024]{4,3,1,2,0:T(2,128)} %copy.149), calls=%async_computation.3 | async-start | bytes 8388608 | tf_op jit(solution)/shard_map/all_to_all | solution.py:65
  110.6 88.6 %all-to-all-done.3 = f32[128,2,2,2,1024]{4,3,1,2,0:T(2,128)} async-done(((f32[128,2,2,2,1024]{4,3,1,2,0:T(2,128)}), f32[128,2,2,2,1024]{4,3,1,2,0:T(2,128)}, u32[]{:S(2)}, u32[]{:S(2)}) %all-to-all-start.3) | async-done | bytes 4194336 | tf_op jit(solution)/shard_map/all_to_all | solution.py:65
  199.2 4.2 copy.150
  209.8 4.1 copy.213
  213.9 5.1 fusion.3
  229.8 8.1 all-to-all-start.6
  242.2 7.7 all-to-all-done.6
  255.5 4.6 all-to-all-start.7
  263.3 7.4 all-to-all-done.7
  270.8 4.7 all-to-all-start.4
  276.8 44.4 %all-to-all-done.4 = f32[128,2,2,1024]{3,1,2,0:T(2,128)S(1)} async-done(((f32[128,2,2,1024]{3,1,2,0:T(2,128)}), f32[128,2,2,1024]{3,1,2,0:T(2,128)S(1)}, u32[]{:S(2)}, u32[]{:S(2)}) %all-to-all-start.4) | async-done | bytes 2097184 | tf_op jit(solution)/shard_map/all_to_all | solution.py:65
  321.2 5.0 all-to-all-start.8
  334.5 6.7 all-to-all-start.5
  341.2 29.2 %all-to-all-done.5 = f32[64,2,2,1024]{3,1,2,0:T(2,128)S(1)} async-done(((f32[64,2,2,1024]{3,1,2,0:T(2,128)}), f32[64,2,2,1024]{3,1,2,0:T(2,128)S(1)}, u32[]{:S(2)}, u32[]{:S(2)}) %all-to-all-start.5) | async-done | bytes 1048608 | tf_op jit(solution)/shard_map/all_to_all | solution.py:65
  375.9 5.4 fusion.16
  390.2 3.8 fusion.18
  395.2 525.0 %all-reduce.2.cloned.1.call-done = f32[3,7,1024]{2,0,1:T(4,128)} async-done(((f32[3,7,1024]{2,0,1:T(4,128)}), f32[3,7,1024]{2,0,1:T(4,128)}) %all-reduce.2.cloned.1.call-update) | async-done | bytes 86032 | tf_op jit(solution)/shard_map/psum | solution.py:172
  (139 shorter events, 80.5 us)
Async XLA Ops:
  7.2 21.5 %copy-start.2 = (bf16[128,3,1024]{2,0,1:T(8,128)(2,1)S(1)}, bf16[128,3,1024]{2,0,1:T(8,128)(2,1)}, u32[]{:S(2)}) copy-start(bf16[128,3,1024]{2,0,1:T(8,128)(2,1)} %param.4) | copy-start | bytes 2359300
  8.1 18.6 %collective-permute-start = (bf16[6,3,1024]{2,1,0:T(4,128)(2,1)S(1)}, bf16[6,3,1024]{2,1,0:T(4,128)(2,1)S(1)}, u32[]{:S(2)}, u32[]{:S(2)}) collective-permute-start(bf16[6,3,1024]{2,1,0:T(4,128)(2,1)S(1)} %copy.248), channel_id=1, source_target_pairs={{0,4},{4,8},{8,12},{12,16},{16,20},{20,24},{24,28},{28,32},{32,36}... | collective-permute-start | bytes 110600 | tf_op jit(solution)/shard_map/ppermute | solution.py:13
  13.4 24.6 %all-to-all-start = ((f32[128,1,2]{2,1,0:T(1,128)}), f32[128,1,2]{2,1,0:T(1,128)S(1)}, u32[]{:S(2)}, u32[]{:S(2)}) async-start(f32[128,1,2]{2,1,0:T(1,128)} %bitcast.9), calls=%async_computation | async-start | bytes 131072 | tf_op jit(solution)/shard_map/all_to_all | solution.py:66
  26.7 7.6 copy-start.11
  34.3 1.4 copy-start.1
  34.3 1.4 copy-start.8
  38.0 39.1 %all-to-all-start.2 = ((f32[128,1,2,1024]{3,2,1,0:T(2,128)}), f32[128,1,2,1024]{3,2,1,0:T(2,128)S(1)}, u32[]{:S(2)}, u32[]{:S(2)}) async-start(f32[128,1,2,1024]{3,2,1,0:T(2,128)} %copy.147), calls=%async_computation.2 | async-start | bytes 2097152 | tf_op jit(solution)/shard_map/all_to_all | solution.py:65
  50.0 36.0 %copy-start.13 = (f32[128,2]{0,1:T(2,128)}, f32[128,2]{0,1:T(2,128)S(1)}, u32[]{:S(2)}) copy-start(f32[128,2]{0,1:T(2,128)S(1)} %get-tuple-element.73) | copy-start | bytes 3076
  77.1 18.8 %all-to-all-start.1 = ((f32[128,2,2,2]{3,1,2,0:T(2,128)}), f32[128,2,2,2]{3,1,2,0:T(2,128)S(1)}, u32[]{:S(2)}, u32[]{:S(2)}) async-start(f32[128,2,2,2]{3,1,2,0:T(2,128)} %copy.137), calls=%async_computation.1 | async-start | bytes 524288 | tf_op jit(solution)/shard_map/all_to_all | solution.py:66
  95.8 103.3 %all-to-all-start.3 = ((f32[128,2,2,2,1024]{4,3,1,2,0:T(2,128)}), f32[128,2,2,2,1024]{4,3,1,2,0:T(2,128)}, u32[]{:S(2)}, u32[]{:S(2)}) async-start(f32[128,2,2,2,1024]{4,3,1,2,0:T(2,128)} %copy.149), calls=%async_computation.3 | async-start | bytes 8388608 | tf_op jit(solution)/shard_map/all_to_all | solution.py:65
  222.2 3.8 copy-start.6
  222.2 3.8 copy-start.7
  229.8 20.1 %all-to-all-start.6 = ((f32[128,2,2,2]{3,1,2,0:T(2,128)}), f32[128,2,2,2]{3,1,2,0:T(2,128)}, u32[]{:S(2)}, u32[]{:S(2)}) async-start(f32[128,2,2,2]{3,1,2,0:T(2,128)} %copy.168), calls=%async_computation.6 | async-start | bytes 524288 | tf_op jit(solution)/shard_map/all_to_all | solution.py:66
  239.9 2.0 copy-start.14
  239.9 2.0 copy-start.15
  255.5 15.3 %all-to-all-start.7 = ((f32[64,2,2]{2,1,0:T(2,128)}), f32[64,2,2]{2,1,0:T(2,128)S(1)}, u32[]{:S(2)}, u32[]{:S(2)}) async-start(f32[64,2,2]{2,1,0:T(2,128)} %copy.173), calls=%async_computation.7 | async-start | bytes 131072 | tf_op jit(solution)/shard_map/all_to_all | solution.py:66
  270.8 50.4 %all-to-all-start.4 = ((f32[128,2,2,1024]{3,1,2,0:T(2,128)}), f32[128,2,2,1024]{3,1,2,0:T(2,128)S(1)}, u32[]{:S(2)}, u32[]{:S(2)}) async-start(f32[128,2,2,1024]{3,1,2,0:T(2,128)} %copy.156), calls=%async_computation.4 | async-start | bytes 4194304 | tf_op jit(solution)/shard_map/all_to_all | solution.py:65
  321.2 13.3 %all-to-all-start.8 = ((f32[2,4,32]{2,0,1:T(2,128)}), f32[2,4,32]{2,0,1:T(2,128)S(1)}, u32[]{:S(2)}, u32[]{:S(2)}) async-start(f32[2,4,32]{2,0,1:T(2,128)} %copy.176), calls=%async_computation.8 | async-start | bytes 8192 | tf_op jit(solution)/shard_map/all_to_all | solution.py:155
  334.5 35.9 %all-to-all-start.5 = ((f32[64,2,2,1024]{3,1,2,0:T(2,128)}), f32[64,2,2,1024]{3,1,2,0:T(2,128)S(1)}, u32[]{:S(2)}, u32[]{:S(2)}) async-start(f32[64,2,2,1024]{3,1,2,0:T(2,128)} %copy.159), calls=%async_computation.5 | async-start | bytes 2097152 | tf_op jit(solution)/shard_map/all_to_all | solution.py:65
  341.1 579.1 %all-reduce.2.cloned.1.call-start = ((), (), s32[]{:S(2)}) async-start(), calls=%async_computation.9 | async-start | bytes 229376 | tf_op jit(solution)/shard_map/psum | solution.py:172
  370.9 3.5 copy-start.5
  371.8 3.4 copy-start.9
  382.8 6.0 collective-permute-start.1
  384.3 5.9 copy-start.12
  (4 other events, 4.1 us)
Sparse Core Ops, SparseCore 0:
  385.2 534.9 all-reduce.1
where the time goes:
time: 937 us; the launch traced here: 929 us
  waiting for transfers between devices  733 us (78%)
  starting transfers between devices  74.5 us (8%)
  local copies, waits for them, and re-layouts  57.2 us (6%)
  other arithmetic  34.2 us (4%)
  matrix products  16 us (2%)
  between operations  15 us (2%)
    psum x1, waiting for transfers between devices, local(): lax.psum(jnp.stack(short_terms, 1), 'seq') * (1.0 / math.sqrt(token_count))  525 us
    all_to_all x4, waiting for transfers between devices, transpose_pair(): lax.all_to_all(signals, 'seq', split_axis=0, concat_axis=1, tiled=True)  188 us
    all_to_all x4, starting transfers between devices, transpose_pair(): lax.all_to_all(signals, 'seq', split_axis=0, concat_axis=1, tiled=True)  33.2 us
    all_to_all x4, starting transfers between devices, transpose_pair(): lax.all_to_all(filters, 'seq', split_axis=0, concat_axis=1, tiled=True)  30.9 us
  transfers between devices with their start and end apart: 12, of which 9 were waited for; matrix products, arithmetic and copies ran while one was open for 6% of the time, Pallas kernels for 0%

commit v1 on v0

--- a/solution.py
+++ b/solution.py
@@ -169,7 +169,9 @@
         short_terms.append(
             jnp.sum(feat_grad * extended[first_row : first_row + row_count].astype(jnp.float32), 0)
         )
-    grad_short = lax.psum(jnp.stack(short_terms, 1), "seq") * (1.0 / math.sqrt(token_count))
+    grad_short = jnp.sum(lax.all_gather(jnp.stack(short_terms, 1), "seq"), axis=0) * (
+        1.0 / math.sqrt(token_count)
+    )
     return (grad_proj.astype(jnp.bfloat16), grad_short, owned_grad)
 
 

time: 937 us -> 662 us (0.71)
  waiting for transfers between devices: 733 us -> 406 us
  blocking collectives: 0 us -> 73.9 us
  starting transfers between devices: 74.5 us -> 53 us
    psum x1 -> x0, waiting for transfers between devices: 525 us -> none  [local(): lax.psum(jnp.stack(short_terms, 1), 'seq') * (1.0 / math.sqrt(token_count))]
    all_gather x0 -> x1, waiting for transfers between devices: none -> 243 us  [local(): lax.all_gather(jnp.stack(short_terms, 1), 'seq')]
    all_to_all x0 -> x4, blocking collectives: none -> 73.9 us  [the longest x2 35.4 us: transpose_pair(): lax.all_to_all(filters, 'seq', split_axis=0, concat_axis=1, tiled=True)]
    all_to_all x4 -> x3, waiting for transfers between devices: 188 us -> 162 us  [transpose_pair(): lax.all_to_all(signals, 'seq', split_axis=0, concat_axis=1, tiled=True)]
    all_to_all x4 -> x2, waiting for transfers between devices: 16.3 us -> 1.14 us  [transpose_pair(): lax.all_to_all(filters, 'seq', split_axis=0, concat_axis=1, tiled=True)]
    all_to_all x4 -> x2, starting transfers between devices: 30.9 us -> 18.2 us  [transpose_pair(): lax.all_to_all(filters, 'seq', split_axis=0, concat_axis=1, tiled=True)]
    all_to_all x4 -> x3, starting transfers between devices: 33.2 us -> 29.4 us  [transpose_pair(): lax.all_to_all(signals, 'seq', split_axis=0, concat_axis=1, tiled=True)]
  transfers between devices with their start and end apart: 12 -> 8, of which waited for: 9 -> 5; matrix products, arithmetic and copies ran while one was open for 6% -> 7% of each run, Pallas kernels for 0% -> 0%
where the time goes in v1:
time: 662 us; the launch traced here: 654 us
  waiting for transfers between devices  406 us (61%)
  blocking collectives  73.9 us (11%)
  local copies, waits for them, and re-layouts  55.5 us (8%)
  starting transfers between devices  53 us (8%)
  other arithmetic  35 us (5%)
  matrix products  15.3 us (2%)
  between operations  15.2 us (2%)
    all_gather x1, waiting for transfers between devices, local(): lax.all_gather(jnp.stack(short_terms, 1), 'seq')  243 us
    all_to_all x3, waiting for transfers between devices, transpose_pair(): lax.all_to_all(signals, 'seq', split_axis=0, concat_axis=1, tiled=True)  162 us
    all_to_all x2, blocking collectives, transpose_pair(): lax.all_to_all(filters, 'seq', split_axis=0, concat_axis=1, tiled=True)  35.4 us
    all_to_all x1, blocking collectives, transpose_pair(): lax.all_to_all(signals, 'seq', split_axis=0, concat_axis=1, tiled=True)  31.9 us
    all_to_all x3, starting transfers between devices, transpose_pair(): lax.all_to_all(signals, 'seq', split_axis=0, concat_axis=1, tiled=True)  29.4 us
    all_to_all x2, starting transfers between devices, transpose_pair(): lax.all_to_all(filters, 'seq', split_axis=0, concat_axis=1, tiled=True)  18.2 us
  transfers between devices with their start and end apart: 8, of which 5 were waited for; matrix products, arithmetic and copies ran while one was open for 7% of the time, Pallas kernels for 0%

profile of v1, /device:TPU:16, one launch (start us, length us, event | category | flops | bytes accessed | tf_op | source)
XLA Modules:
  0.0 654.1 jit_solution(13811315159614352652)
XLA Ops:
  8.1 3.8 collective-permute-start
  13.4 11.8 %all-to-all-start = ((f32[128,1,2]{2,1,0:T(1,128)}), f32[128,1,2]{2,1,0:T(1,128)S(1)}, u32[]{:S(2)}, u32[]{:S(2)}) async-start(f32[128,1,2]{2,1,0:T(1,128)} %bitcast.9), calls=%async_computation | async-start | bytes 131072 | tf_op jit(solution)/shard_map/all_to_all | solution.py:66
  28.7 5.6 fusion.9
  38.0 11.2 %all-to-all-start.2 = ((f32[128,1,2,1024]{3,2,1,0:T(2,128)}), f32[128,1,2,1024]{3,2,1,0:T(2,128)S(1)}, u32[]{:S(2)}, u32[]{:S(2)}) async-start(f32[128,1,2,1024]{3,2,1,0:T(2,128)} %copy.144), calls=%async_computation.2 | async-start | bytes 2097152 | tf_op jit(solution)/shard_map/all_to_all | solution.py:65
  51.0 26.1 %all-to-all-done.2 = f32[128,1,2,1024]{3,2,1,0:T(2,128)S(1)} async-done(((f32[128,1,2,1024]{3,2,1,0:T(2,128)}), f32[128,1,2,1024]{3,2,1,0:T(2,128)S(1)}, u32[]{:S(2)}, u32[]{:S(2)}) %all-to-all-start.2) | async-done | bytes 1048608 | tf_op jit(solution)/shard_map/all_to_all | solution.py:65
  77.1 6.5 all-to-all-start.1
  89.5 5.3 copy.146
  95.9 10.5 %all-to-all-start.3 = ((f32[128,2,2,2,1024]{4,3,1,2,0:T(2,128)}), f32[128,2,2,2,1024]{4,3,1,2,0:T(2,128)}, u32[]{:S(2)}, u32[]{:S(2)}) async-start(f32[128,2,2,2,1024]{4,3,1,2,0:T(2,128)} %copy.146), calls=%async_computation.3 | async-start | bytes 8388608 | tf_op jit(solution)/shard_map/all_to_all | solution.py:65
  109.9 89.2 %all-to-all-done.3 = f32[128,2,2,2,1024]{4,3,1,2,0:T(2,128)} async-done(((f32[128,2,2,2,1024]{4,3,1,2,0:T(2,128)}), f32[128,2,2,2,1024]{4,3,1,2,0:T(2,128)}, u32[]{:S(2)}, u32[]{:S(2)}) %all-to-all-start.3) | async-done | bytes 4194336 | tf_op jit(solution)/shard_map/all_to_all | solution.py:65
  199.1 4.2 copy.147
  203.3 3.7 fusion.141
  209.7 4.5 copy.209
  214.2 5.1 fusion.3
  227.5 7.7 %all-to-all-start.4 = ((f32[128,2,2,1024]{3,1,2,0:T(2,128)}), f32[128,2,2,1024]{3,1,2,0:T(2,128)}, u32[]{:S(2)}, u32[]{:S(2)}) async-start(f32[128,2,2,1024]{3,1,2,0:T(2,128)} %copy.153), calls=%async_computation.4 | async-start | bytes 4194304 | tf_op jit(solution)/shard_map/all_to_all | solution.py:65
  236.2 47.0 %all-to-all-done.4 = f32[128,2,2,1024]{3,1,2,0:T(2,128)} async-done(((f32[128,2,2,1024]{3,1,2,0:T(2,128)}), f32[128,2,2,1024]{3,1,2,0:T(2,128)}, u32[]{:S(2)}, u32[]{:S(2)}) %all-to-all-start.4) | async-done | bytes 2097184 | tf_op jit(solution)/shard_map/all_to_all | solution.py:65
  283.1 3.7 copy.248
  286.9 3.8 all_to_all.127
  294.6 31.9 %all_to_all.148 = f32[64,2,2,1024]{3,1,2,0:T(2,128)S(1)} all-to-all(f32[64,2,2,1024]{3,1,2,0:T(2,128)S(1)} %copy.156), channel_id=1, replica_groups=mesh['seq'=64,'ch'=4] {'seq'}, dimensions={0} | all-to-all | bytes 2097152 | tf_op jit(solution)/shard_map/all_to_all | solution.py:65
  332.1 5.3 fusion.16
  344.8 18.8 %all_to_all.149 = f32[128,2,2,2]{3,1,2,0:T(2,128)S(1)} all-to-all(f32[128,2,2,2]{3,1,2,0:T(2,128)S(1)} %copy.165), channel_id=1, replica_groups=mesh['seq'=64,'ch'=4] {'seq'}, dimensions={0} | all-to-all | bytes 8192 | tf_op jit(solution)/shard_map/all_to_all | solution.py:66
  366.3 16.7 %all_to_all.150 = f32[64,2,2]{2,1,0:T(2,128)S(1)} all-to-all(f32[64,2,2]{2,1,0:T(2,128)S(1)} %copy.170), channel_id=1, replica_groups=mesh['seq'=64,'ch'=4] {'seq'}, dimensions={0} | all-to-all | bytes 2048 | tf_op jit(solution)/shard_map/all_to_all | solution.py:66
  386.4 6.6 %all_to_all.151 = f32[2,4,32]{2,0,1:T(2,128)S(1)} all-to-all(f32[2,4,32]{2,0,1:T(2,128)S(1)} %copy.173), channel_id=1, replica_groups=mesh['seq'=64,'ch'=4] {'ch'}, dimensions={1} | all-to-all | bytes 2048 | tf_op jit(solution)/shard_map/all_to_all | solution.py:155
  394.5 3.8 fusion.18
  399.5 242.9 %all-gather.3.cloned.1.call-done = f32[192,7,1024]{2,1,0:T(8,128)} async-done(((f32[3,7,1024]{2,1,0:T(8,128)}), f32[192,7,1024]{2,1,0:T(8,128)}) %all-gather.3.cloned.1.call-update) | async-done | bytes 5505040 | tf_op jit(solution)/shard_map/all_gather | solution.py:172
  (166 shorter events, 63.4 us)
Async XLA Ops:
  7.2 21.5 %copy-start.8 = (bf16[128,3,1024]{2,0,1:T(8,128)(2,1)S(1)}, bf16[128,3,1024]{2,0,1:T(8,128)(2,1)}, u32[]{:S(2)}) copy-start(bf16[128,3,1024]{2,0,1:T(8,128)(2,1)} %param.4) | copy-start | bytes 2359300
  8.1 18.6 %collective-permute-start = (bf16[6,3,1024]{2,1,0:T(4,128)(2,1)S(1)}, bf16[6,3,1024]{2,1,0:T(4,128)(2,1)S(1)}, u32[]{:S(2)}, u32[]{:S(2)}) collective-permute-start(bf16[6,3,1024]{2,1,0:T(4,128)(2,1)S(1)} %copy.244), channel_id=1, source_target_pairs={{0,4},{4,8},{8,12},{12,16},{16,20},{20,24},{24,28},{28,32},{32,36}... | collective-permute-start | bytes 110600 | tf_op jit(solution)/shard_map/ppermute | solution.py:13
  13.4 24.7 %all-to-all-start = ((f32[128,1,2]{2,1,0:T(1,128)}), f32[128,1,2]{2,1,0:T(1,128)S(1)}, u32[]{:S(2)}, u32[]{:S(2)}) async-start(f32[128,1,2]{2,1,0:T(1,128)} %bitcast.9), calls=%async_computation | async-start | bytes 131072 | tf_op jit(solution)/shard_map/all_to_all | solution.py:66
  26.7 7.6 %copy-start.17 = (f32[3,1024]{1,0:T(4,128)}, f32[3,1024]{1,0:T(4,128)S(1)}, u32[]{:S(2)}) copy-start(f32[3,1024]{1,0:T(4,128)S(1)} %get-tuple-element.76) | copy-start | bytes 36868
  26.7 7.6 %copy-start.19 = (f32[3,1024]{1,0:T(4,128)}, f32[3,1024]{1,0:T(4,128)S(1)}, u32[]{:S(2)}) copy-start(f32[3,1024]{1,0:T(4,128)S(1)} %get-tuple-element.77) | copy-start | bytes 36868
  26.7 7.6 %copy-start.21 = (f32[3,1024]{1,0:T(4,128)}, f32[3,1024]{1,0:T(4,128)S(1)}, u32[]{:S(2)}) copy-start(f32[3,1024]{1,0:T(4,128)S(1)} %get-tuple-element.74) | copy-start | bytes 36868
  26.7 7.6 %copy-start.23 = (f32[3,1024]{1,0:T(4,128)}, f32[3,1024]{1,0:T(4,128)S(1)}, u32[]{:S(2)}) copy-start(f32[3,1024]{1,0:T(4,128)S(1)} %get-tuple-element.75) | copy-start | bytes 36868
  26.7 7.6 %copy-start.25 = (f32[3,1,1024]{2,0,1:T(4,128)}, f32[3,1,1024]{2,0,1:T(4,128)S(1)}, u32[]{:S(2)}) copy-start(f32[3,1,1024]{2,0,1:T(4,128)S(1)} %copy.249) | copy-start | bytes 36868
  38.0 39.1 %all-to-all-start.2 = ((f32[128,1,2,1024]{3,2,1,0:T(2,128)}), f32[128,1,2,1024]{3,2,1,0:T(2,128)S(1)}, u32[]{:S(2)}, u32[]{:S(2)}) async-start(f32[128,1,2,1024]{3,2,1,0:T(2,128)} %copy.144), calls=%async_computation.2 | async-start | bytes 2097152 | tf_op jit(solution)/shard_map/all_to_all | solution.py:65
  49.4 174.5 %copy-start.27 = (f32[128,2]{0,1:T(2,128)}, f32[128,2]{0,1:T(2,128)S(1)}, u32[]{:S(2)}) copy-start(f32[128,2]{0,1:T(2,128)S(1)} %get-tuple-element.73) | copy-start | bytes 3076
  49.4 174.5 %copy-start.29 = (f32[128,2]{0,1:T(2,128)}, f32[128,2]{0,1:T(2,128)S(1)}, u32[]{:S(2)}) copy-start(f32[128,2]{0,1:T(2,128)S(1)} %get-tuple-element.71) | copy-start | bytes 3076
  77.1 18.8 %all-to-all-start.1 = ((f32[128,2,2,2]{3,1,2,0:T(2,128)}), f32[128,2,2,2]{3,1,2,0:T(2,128)S(1)}, u32[]{:S(2)}, u32[]{:S(2)}) async-start(f32[128,2,2,2]{3,1,2,0:T(2,128)} %copy.134), calls=%async_computation.1 | async-start | bytes 524288 | tf_op jit(solution)/shard_map/all_to_all | solution.py:66
  95.9 103.2 %all-to-all-start.3 = ((f32[128,2,2,2,1024]{4,3,1,2,0:T(2,128)}), f32[128,2,2,2,1024]{4,3,1,2,0:T(2,128)}, u32[]{:S(2)}, u32[]{:S(2)}) async-start(f32[128,2,2,2,1024]{4,3,1,2,0:T(2,128)} %copy.146), calls=%async_computation.3 | async-start | bytes 8388608 | tf_op jit(solution)/shard_map/all_to_all | solution.py:65
  227.5 55.7 %all-to-all-start.4 = ((f32[128,2,2,1024]{3,1,2,0:T(2,128)}), f32[128,2,2,1024]{3,1,2,0:T(2,128)}, u32[]{:S(2)}, u32[]{:S(2)}) async-start(f32[128,2,2,1024]{3,1,2,0:T(2,128)} %copy.153), calls=%async_computation.4 | async-start | bytes 4194304 | tf_op jit(solution)/shard_map/all_to_all | solution.py:65
  235.2 407.2 %all-gather.3.cloned.1.call-start = ((), (), s32[]{:S(2)}) async-start(), calls=%async_computation.9 | async-start | bytes 6389760 | tf_op jit(solution)/shard_map/all_gather | solution.py:172
  341.5 41.6 %copy-start.2 = (f32[128,1,1024]{2,1,0:T(1,128)S(1)}, f32[128,1,1024]{2,1,0:T(1,128)}, u32[]{:S(2)}) copy-start(f32[128,1,1024]{2,1,0:T(1,128)} %copy-done.1) | copy-start | bytes 1572868
  341.5 41.6 %copy-start.4 = (f32[128,1,1024]{2,1,0:T(1,128)S(1)}, f32[128,1,1024]{2,1,0:T(1,128)}, u32[]{:S(2)}) copy-start(f32[128,1,1024]{2,1,0:T(1,128)} %copy-done.3) | copy-start | bytes 1572868
  341.5 41.6 %copy-start.6 = (f32[128,1,1024]{2,1,0:T(1,128)S(1)}, f32[128,1,1024]{2,1,0:T(1,128)}, u32[]{:S(2)}) copy-start(f32[128,1,1024]{2,1,0:T(1,128)} %copy-done.5) | copy-start | bytes 1572868
  384.6 9.9 %copy-start.18 = (f32[3,1024]{1,0:T(4,128)S(1)}, f32[3,1024]{1,0:T(4,128)}, u32[]{:S(2)}) copy-start(f32[3,1024]{1,0:T(4,128)} %copy-done.17) | copy-start | bytes 36868
  384.6 9.9 %copy-start.20 = (f32[3,1024]{1,0:T(4,128)S(1)}, f32[3,1024]{1,0:T(4,128)}, u32[]{:S(2)}) copy-start(f32[3,1024]{1,0:T(4,128)} %copy-done.19) | copy-start | bytes 36868
  384.6 9.9 %copy-start.22 = (f32[3,1024]{1,0:T(4,128)S(1)}, f32[3,1024]{1,0:T(4,128)}, u32[]{:S(2)}) copy-start(f32[3,1024]{1,0:T(4,128)} %copy-done.21) | copy-start | bytes 36868
  384.6 9.9 %copy-start.24 = (f32[3,1024]{1,0:T(4,128)S(1)}, f32[3,1024]{1,0:T(4,128)}, u32[]{:S(2)}) copy-start(f32[3,1024]{1,0:T(4,128)} %copy-done.23) | copy-start | bytes 36868
  384.7 9.9 %copy-start.26 = (f32[3,1,1024]{2,0,1:T(4,128)S(1)}, f32[3,1,1024]{2,0,1:T(4,128)}, u32[]{:S(2)}) copy-start(f32[3,1,1024]{2,0,1:T(4,128)} %copy-done.25) | copy-start | bytes 36868
  384.7 8.4 %collective-permute-start.1 = (bf16[6,3,1024]{2,1,0:T(4,128)(2,1)S(1)}, bf16[6,3,1024]{2,1,0:T(4,128)(2,1)S(1)}, u32[]{:S(2)}, u32[]{:S(2)}) collective-permute-start(bf16[6,3,1024]{2,1,0:T(4,128)(2,1)S(1)} %slice.341), channel_id=1, source_target_pairs={{4,0},{8,4},{12,8},{16,12},{20,16},{24,20},{28,24},{32,28},{36,32}... | collective-permute-start | bytes 110600 | tf_op jit(solution)/shard_map/ppermute | solution.py:13
  (15 other events, 35.8 us)
Sparse Core Ops, SparseCore 0:
  338.5 303.8 all-gather.2
